TPU v7x, 256 devices: a whole 4x4x8 slice. The times are simulated.
256 devices in a mesh: row: 16 (over z, y_lo), col: 16 (over y_hi, x, core).
Axes of the slice: x: 4, y: 4 (y_hi: 2, y_lo: 2; y = y_hi * 2 + y_lo), z: 8, core: 2. Of those that a mesh axis runs over, the one named last changes fastest.
Arguments:
- ancestor: float32 [8192, 8192], P('row', 'col'), may hold values from -0.0625 to 0.0625
- factor: float32 [8192, 16, 128], P(('row', 'col')), may hold values from -1.5 to 1.5
- diag_inv: float32 [16, 128, 128], replicated, may hold values from -6 to 6
- structure: int32 [16, 768], replicated, may hold values from 0 to 1023, as said below
Outputs:
- inverse_panel: float32 [8192, 16, 128], P(('row', 'col'))
- inverse_diagonal: float32 [16, 128, 128], replicated
Inputs may be any that keep to these rules, and one draw needn't show every extreme that they name: Each row of structure lists 768 different block numbers, in no particular order.
All inputs are finite; a program needn't handle non-finite values.
Results may differ from a plain program's by a relative error of at most 0.00007.
Values sent between devices are 32-bit elements; how exact they have to be, the bound alone decides.
No kernel may reach another device: no remote copies, remote signals or barrier semaphores. Data moves between devices by JAX's collectives and lax.ppermute only.
A program may use at most 64 MiB of HBM per device.

v0:
```python
import jax
import jax.numpy as jnp
from jax import lax
from jax.sharding import PartitionSpec as P

RB = 8


def spread_2(value, axis, source):
    kept = jnp.where(lax.axis_index(axis) == source, value, 0).astype(value.dtype)
    return lax.psum(kept, axis)


def per_device(ancestor, factor, diag_inv, structure):
    row_devices = lax.axis_size("row")
    col_devices = lax.axis_size("col")
    ratio = row_devices // col_devices
    local_rows = factor.shape[0]
    width = factor.shape[2]
    first_row = (lax.axis_index("row") * col_devices + lax.axis_index("col")) * local_rows
    block_ids = (first_row + jnp.arange(local_rows, dtype=jnp.int32)) // RB
    matches = block_ids[:, None, None] == structure[None, :, :]
    row_mask = jnp.any(matches, axis=2).astype(jnp.float32)
    masked = factor * row_mask[:, :, None]
    count_sib = masked.shape[1]
    spread = masked.reshape(local_rows, count_sib * width)
    block_row = lax.all_gather(spread, "col", axis=0, tiled=True)
    received = spread_2(block_row, "row", lax.axis_index("col") * ratio + 0)
    summed = lax.psum_scatter(
        jnp.dot(
            ancestor, received, precision=lax.Precision.HIGHEST, preferred_element_type=jnp.float32
        ),
        "col",
        scatter_dimension=0,
        tiled=True,
    )
    panel = -summed.reshape(local_rows, count_sib, width)
    panel = panel * row_mask[:, :, None]
    local_update = jnp.einsum("bsw,bsv->swv", masked, panel, precision=lax.Precision.HIGHEST)
    total_update = lax.psum(local_update, ("row", "col"))
    return (panel, diag_inv - total_update)


def solution(mesh):
    placed = (P("row", "col"), P(("row", "col"), None, None), P(), P())
    return jax.shard_map(
        per_device,
        mesh=mesh,
        in_specs=placed,
        out_specs=(P(("row", "col"), None, None), P()),
        check_vma=False,
    )
```

profile of v0, /device:TPU:2, one launch (start us, length us, event | category | flops | bytes accessed | tf_op | source)
XLA Modules:
  0.0 657.8 jit_solution(703054387542532473)
XLA Ops:
  7.2 0.0 copy-start
  7.2 0.0 all-gather.2.cloned.1.call-start
  7.2 1.6 compare_reduce_fusion
  8.8 1.1 broadcast_multiply_fusion.1
  9.9 0.8 copy.23
  10.7 0.0 all-gather.2.cloned.1.call-update
  10.7 0.0 all-reduce.3.cloned.1.call-start
  10.8 64.4 %all-gather.2.cloned.1.call-done = f32[512,2048]{1,0:T(8,128)} async-done(((f32[32,2048]{1,0:T(8,128)}), f32[512,2048]{1,0:T(8,128)}) %all-gather.2.cloned.1.call-update) | async-done | bytes 4194320 | tf_op jit(solution)/shard_map/all_gather | solution.py:27
  75.2 2.5 broadcast_select_fusion
  77.7 0.0 all-reduce.3.cloned.1.call-update
  77.7 0.0 reduce-scatter.4.cloned.1.call-start
  77.8 199.0 %all-reduce.3.cloned.1.call-done = f32[512,2048]{1,0:T(8,128)} async-done(((f32[512,2048]{1,0:T(8,128)}), f32[512,2048]{1,0:T(8,128)}) %all-reduce.3.cloned.1.call-update) | async-done | bytes 4194320 | tf_op jit(solution)/shard_map/psum | solution.py:11
  276.8 0.0 copy-done
  276.8 16.3 %convolution_bitcast_fusion = f32[512,2048]{0,1:T(8,128)} fusion(f32[512,2048]{1,0:T(8,128)} %all-reduce.3.cloned.1.call-done, f32[512,512]{1,0:T(8,128)S(1)} %copy-done), kind=kOutput, calls=%fused_computation | convolution fusion | flops 6442450944 | bytes 9437184 | tf_op jit(solution)/shard_map/dot_general | solution.py:30
  293.0 5.4 copy.15
  298.4 0.0 reduce-scatter.4.cloned.1.call-update
  298.5 0.0 all-reduce.5.cloned.1.call-start
  298.5 88.3 %reduce-scatter.4.cloned.1.call-done = f32[32,2048]{1,0:T(8,128)} async-done(((f32[512,2048]{1,0:T(8,128)}), f32[32,2048]{1,0:T(8,128)}) %reduce-scatter.4.cloned.1.call-update) | async-done | bytes 262160
  386.8 1.3 copy.16
  388.1 0.1 neg.6
  388.2 0.3 copy.12
  388.5 0.1 broadcast_multiply_fusion
  388.7 0.0 copy-start.1
  388.7 2.8 fusion
  391.5 0.0 all-reduce.5.cloned.1.call-update
  391.5 257.1 %all-reduce.5.cloned.1.call-done = f32[16,128,128]{2,1,0:T(8,128)} async-done(((f32[16,128,128]{2,1,0:T(8,128)}), f32[16,128,128]{2,1,0:T(8,128)}) %all-reduce.5.cloned.1.call-update) | async-done | bytes 1048592 | tf_op jit(solution)/shard_map/psum | solution.py:40
  648.6 2.6 sub.10
  651.3 0.0 copy-done.1
  (2 shorter events, 0.0 us)
Async XLA Ops:
  7.2 269.6 %copy-start = (f32[512,512]{1,0:T(8,128)S(1)}, f32[512,512]{1,0:T(8,128)}, u32[]{:S(2)}) copy-start(f32[512,512]{1,0:T(8,128)} %param.4) | copy-start | bytes 3145732
  7.2 68.0 %all-gather.2.cloned.1.call-start = ((), (), s32[]{:S(2)}) async-start(), calls=%async_computation.1 | async-start | bytes 4456448 | tf_op jit(solution)/shard_map/all_gather | solution.py:27
  10.7 266.0 %all-reduce.3.cloned.1.call-start = ((), (), s32[]{:S(2)}) async-start(), calls=%async_computation.2 | async-start | bytes 8388608 | tf_op jit(solution)/shard_map/psum | solution.py:11
  77.7 309.1 %reduce-scatter.4.cloned.1.call-start = ((), (), s32[]{:S(2)}) async-start(), calls=%async_computation.4 | async-start | bytes 4456448
  298.5 350.2 %all-reduce.5.cloned.1.call-start = ((), (), s32[]{:S(2)}) async-start(), calls=%async_computation.3 | async-start | bytes 2097152 | tf_op jit(solution)/shard_map/psum | solution.py:40
  388.7 262.6 %copy-start.1 = (f32[32,16,128]{2,1,0:T(8,128)}, f32[32,16,128]{2,1,0:T(8,128)S(1)}, u32[]{:S(2)}) copy-start(f32[32,16,128]{2,1,0:T(8,128)S(1)} %broadcast_multiply_fusion) | copy-start | bytes 786436
Sparse Core Ops, SparseCore 0:
  11.3 63.8 all-gather.1
  77.8 198.8 all-reduce.2
  298.6 88.2 reduce-scatter.3
  393.6 254.9 all-reduce.4
where the time goes:
time: 658 us
  waiting for transfers between devices  609 us (93%)
  matrix products  19.1 us (3%)
  between operations  13.8 us (2%)
  other arithmetic  8.03 us (1%)
  local copies, waits for them, and re-layouts  7.8 us (1%)
    psum x1, waiting for transfers between devices, per_device(): total_update = lax.psum(local_update, ('row', 'col'))  257 us
    psum x1, waiting for transfers between devices, spread_2(): return lax.psum(kept, axis)  199 us
    unnamed x5, waiting for transfers between devices  88.4 us
    all_gather x1, waiting for transfers between devices, per_device(): block_row = lax.all_gather(spread, 'col', axis=0, tiled=True)  64.4 us
    dot_general x1, matrix products, per_device(): jnp.dot(ancestor, received, precision=lax.Precision.HIGHEST, preferred_el...  16.3 us
  transfers between devices with their start and end apart: 4, of which 4 were waited for; matrix products, arithmetic and copies ran while one was open for 0% of the time, Pallas kernels for 0%

commit v1 on v0

--- a/solution.py
+++ b/solution.py
@@ -24,7 +24,9 @@
     masked = factor * row_mask[:, :, None]
     count_sib = masked.shape[1]
     spread = masked.reshape(local_rows, count_sib * width)
-    block_row = lax.all_gather(spread, "col", axis=0, tiled=True)
+    block_row = jnp.concatenate(
+        lax.all_to_all(jnp.stack([spread] * lax.axis_size("col")), "col", 0, 0), axis=0
+    )
     received = spread_2(block_row, "row", lax.axis_index("col") * ratio + 0)
     summed = lax.psum_scatter(
         jnp.dot(

time: 658 us -> 663 us (level)
  starting transfers between devices: 0.16 us -> 7.6 us
    all_gather x1 -> x0, waiting for transfers between devices: 64.4 us -> none  [per_device(): block_row = lax.all_gather(spread, 'col', axis=0, tiled=True)]
    all_to_all x0 -> x1, waiting for transfers between devices: none -> 56.9 us  [per_device(): lax.all_to_all(jnp.stack([spread] * lax.axis_size('col')), 'col', 0, 0)]
    all_to_all x0 -> x1, starting transfers between devices: none -> 7.48 us  [per_device(): lax.all_to_all(jnp.stack([spread] * lax.axis_size('col')), 'col', 0, 0)]
    unnamed x5 -> x4, waiting for transfers between devices: 88.4 us -> 88.4 us
where the time goes in v1:
time: 663 us
  waiting for transfers between devices  605 us (91%)
  matrix products  19.1 us (3%)
  between operations  13.8 us (2%)
  local copies, waits for them, and re-layouts  9.63 us (1%)
  other arithmetic  8.03 us (1%)
  starting transfers between devices  7.6 us (1%)
    psum x1, waiting for transfers between devices, per_device(): total_update = lax.psum(local_update, ('row', 'col'))  257 us
    psum x1, waiting for transfers between devices, spread_2(): return lax.psum(kept, axis)  202 us
    unnamed x4, waiting for transfers between devices  88.4 us
    all_to_all x1, waiting for transfers between devices, per_device(): lax.all_to_all(jnp.stack([spread] * lax.axis_size('col')), 'col', 0, 0)  56.9 us
    dot_general x1, matrix products, per_device(): jnp.dot(ancestor, received, precision=lax.Precision.HIGHEST, preferred_el...  16.3 us
  transfers between devices with their start and end apart: 4, of which 4 were waited for; matrix products, arithmetic and copies ran while one was open for 0% of the time, Pallas kernels for 0%

profile of v1, /device:TPU:2, one launch (start us, length us, event | category | flops | bytes accessed | tf_op | source)
XLA Modules:
  0.0 662.8 jit_solution(6437672387634224250)
XLA Ops:
  7.2 0.0 copy-start
  7.2 1.6 compare_reduce_fusion
  8.8 1.1 broadcast_multiply_fusion.1
  9.9 0.1 copy.23
  10.0 2.5 stack.3
  12.4 7.5 %all-to-all-start = ((f32[16,32,2048]{2,1,0:T(8,128)}), f32[16,32,2048]{2,1,0:T(8,128)}, u32[]{:S(2)}, u32[]{:S(2)}) async-start(f32[16,32,2048]{2,1,0:T(8,128)} %stack.3), calls=%async_computation | async-start | bytes 8388608 | tf_op jit(solution)/shard_map/all_to_all | solution.py:28
  19.9 0.0 all-reduce.3.cloned.1.call-start
  20.0 56.9 %all-to-all-done = f32[16,32,2048]{2,1,0:T(8,128)} async-done(((f32[16,32,2048]{2,1,0:T(8,128)}), f32[16,32,2048]{2,1,0:T(8,128)}, u32[]{:S(2)}, u32[]{:S(2)}) %all-to-all-start) | async-done | bytes 4194336 | tf_op jit(solution)/shard_map/all_to_all | solution.py:28
  76.9 2.5 broadcast_select_fusion
  79.4 0.0 all-reduce.3.cloned.1.call-update
  79.4 0.0 reduce-scatter.4.cloned.1.call-start
  79.5 202.0 %all-reduce.3.cloned.1.call-done = f32[512,2048]{1,0:T(8,128)} async-done(((f32[512,2048]{1,0:T(8,128)}), f32[512,2048]{1,0:T(8,128)}) %all-reduce.3.cloned.1.call-update) | async-done | bytes 4194320 | tf_op jit(solution)/shard_map/psum | solution.py:11
  281.5 0.0 copy-done
  281.5 16.3 %convolution_bitcast_fusion = f32[512,2048]{0,1:T(8,128)} fusion(f32[512,2048]{1,0:T(8,128)} %all-reduce.3.cloned.1.call-done, f32[512,512]{1,0:T(8,128)S(1)} %copy-done), kind=kOutput, calls=%fused_computation | convolution fusion | flops 6442450944 | bytes 9437184 | tf_op jit(solution)/shard_map/dot_general | solution.py:32
  297.8 5.5 copy.15
  303.2 0.0 reduce-scatter.4.cloned.1.call-update
  303.2 0.0 all-reduce.5.cloned.1.call-start
  303.3 88.4 %reduce-scatter.4.cloned.1.call-done = f32[32,2048]{1,0:T(8,128)} async-done(((f32[512,2048]{1,0:T(8,128)}), f32[32,2048]{1,0:T(8,128)}) %reduce-scatter.4.cloned.1.call-update) | async-done | bytes 262160
  391.7 1.3 copy.16
  393.0 0.1 neg.6
  393.0 0.3 copy.12
  393.4 0.1 broadcast_multiply_fusion
  393.5 0.0 copy-start.1
  393.5 2.8 fusion
  396.3 0.0 all-reduce.5.cloned.1.call-update
  396.3 257.3 %all-reduce.5.cloned.1.call-done = f32[16,128,128]{2,1,0:T(8,128)} async-done(((f32[16,128,128]{2,1,0:T(8,128)}), f32[16,128,128]{2,1,0:T(8,128)}) %all-reduce.5.cloned.1.call-update) | async-done | bytes 1048592 | tf_op jit(solution)/shard_map/psum | solution.py:42
  653.6 2.6 sub.10
  656.3 0.0 copy-done.1
  (2 shorter events, 0.0 us)
Async XLA Ops:
  7.2 274.3 %copy-start = (f32[512,512]{1,0:T(8,128)S(1)}, f32[512,512]{1,0:T(8,128)}, u32[]{:S(2)}) copy-start(f32[512,512]{1,0:T(8,128)} %param.4) | copy-start | bytes 3145732
  12.4 64.4 %all-to-all-start = ((f32[16,32,2048]{2,1,0:T(8,128)}), f32[16,32,2048]{2,1,0:T(8,128)}, u32[]{:S(2)}, u32[]{:S(2)}) async-start(f32[16,32,2048]{2,1,0:T(8,128)} %stack.3), calls=%async_computation | async-start | bytes 8388608 | tf_op jit(solution)/shard_map/all_to_all | solution.py:28
  19.9 261.6 %all-reduce.3.cloned.1.call-start = ((), (), s32[]{:S(2)}) async-start(), calls=%async_computation.2 | async-start | bytes 8388608 | tf_op jit(solution)/shard_map/psum | solution.py:11
  79.4 312.3 %reduce-scatter.4.cloned.1.call-start = ((), (), s32[]{:S(2)}) async-start(), calls=%async_computation.4 | async-start | bytes 4456448
  303.2 350.4 %all-reduce.5.cloned.1.call-start = ((), (), s32[]{:S(2)}) async-start(), calls=%async_computation.3 | async-start | bytes 2097152 | tf_op jit(solution)/shard_map/psum | solution.py:42
  393.5 262.8 %copy-start.1 = (f32[32,16,128]{2,1,0:T(8,128)}, f32[32,16,128]{2,1,0:T(8,128)S(1)}, u32[]{:S(2)}) copy-start(f32[32,16,128]{2,1,0:T(8,128)S(1)} %broadcast_multiply_fusion) | copy-start | bytes 786436
Sparse Core Ops, SparseCore 0:
  79.5 201.9 all-reduce.2
  303.4 88.2 reduce-scatter.3
  398.6 254.9 all-reduce.4

commit v2 on v0

--- a/solution.py
+++ b/solution.py
@@ -37,7 +37,7 @@
     panel = -summed.reshape(local_rows, count_sib, width)
     panel = panel * row_mask[:, :, None]
     local_update = jnp.einsum("bsw,bsv->swv", masked, panel, precision=lax.Precision.HIGHEST)
-    total_update = lax.psum(local_update, ("row", "col"))
+    total_update = lax.psum(lax.psum(local_update, "col"), "row")
     return (panel, diag_inv - total_update)
 
 

time: 658 us -> 689 us (1.047)
  waiting for transfers between devices: 609 us -> 639 us
    psum x1 -> x2, waiting for transfers between devices: 257 us -> 288 us  [per_device(): total_update = lax.psum(lax.psum(local_update, 'col'), 'row')]
    unnamed x5 -> x6, waiting for transfers between devices: 88.4 us -> 88.4 us
  transfers between devices with their start and end apart: 4 -> 5, of which waited for: 4 -> 5; matrix products, arithmetic and copies ran while one was open for 0% -> 0% of each run, Pallas kernels for 0% -> 0%
where the time goes in v2:
time: 689 us; the launch traced here: 688 us
  waiting for transfers between devices  639 us (93%)
  matrix products  19.1 us (3%)
  between operations  13.9 us (2%)
  other arithmetic  8.03 us (1%)
  local copies, waits for them, and re-layouts  7.8 us (1%)
    psum x2, waiting for transfers between devices, per_device(): total_update = lax.psum(lax.psum(local_update, 'col'), 'row')  288 us
    psum x1, waiting for transfers between devices, spread_2(): return lax.psum(kept, axis)  199 us
    unnamed x6, waiting for transfers between devices  88.4 us
    all_gather x1, waiting for transfers between devices, per_device(): block_row = lax.all_gather(spread, 'col', axis=0, tiled=True)  64.4 us
    dot_general x1, matrix products, per_device(): jnp.dot(ancestor, received, precision=lax.Precision.HIGHEST, preferred_el...  16.3 us
  transfers between devices with their start and end apart: 5, of which 5 were waited for; matrix products, arithmetic and copies ran while one was open for 0% of the time, Pallas kernels for 0%

profile of v2, /device:TPU:2, one launch (start us, length us, event | category | flops | bytes accessed | tf_op | source)
XLA Modules:
  0.0 688.3 jit_solution(5570828117293980589)
XLA Ops:
  7.2 0.0 copy-start
  7.2 0.0 all-gather.2.cloned.1.call-start
  7.2 1.6 compare_reduce_fusion
  8.8 1.1 broadcast_multiply_fusion.1
  9.9 0.8 copy.23
  10.7 0.0 all-gather.2.cloned.1.call-update
  10.7 0.0 all-reduce.4.cloned.1.call-start
  10.8 64.4 %all-gather.2.cloned.1.call-done = f32[512,2048]{1,0:T(8,128)} async-done(((f32[32,2048]{1,0:T(8,128)}), f32[512,2048]{1,0:T(8,128)}) %all-gather.2.cloned.1.call-update) | async-done | bytes 4194320 | tf_op jit(solution)/shard_map/all_gather | solution.py:27
  75.2 2.5 broadcast_select_fusion
  77.7 0.0 all-reduce.4.cloned.1.call-update
  77.7 0.0 reduce-scatter.4.cloned.1.call-start
  77.8 199.0 %all-reduce.4.cloned.1.call-done = f32[512,2048]{1,0:T(8,128)} async-done(((f32[512,2048]{1,0:T(8,128)}), f32[512,2048]{1,0:T(8,128)}) %all-reduce.4.cloned.1.call-update) | async-done | bytes 4194320 | tf_op jit(solution)/shard_map/psum | solution.py:11
  276.8 0.0 copy-done
  276.8 16.3 %convolution_bitcast_fusion = f32[512,2048]{0,1:T(8,128)} fusion(f32[512,2048]{1,0:T(8,128)} %all-reduce.4.cloned.1.call-done, f32[512,512]{1,0:T(8,128)S(1)} %copy-done), kind=kOutput, calls=%fused_computation | convolution fusion | flops 6442450944 | bytes 9437184 | tf_op jit(solution)/shard_map/dot_general | solution.py:30
  293.0 5.4 copy.15
  298.4 0.0 reduce-scatter.4.cloned.1.call-update
  298.5 0.0 all-reduce.6.cloned.1.call-start
  298.5 88.3 %reduce-scatter.4.cloned.1.call-done = f32[32,2048]{1,0:T(8,128)} async-done(((f32[512,2048]{1,0:T(8,128)}), f32[32,2048]{1,0:T(8,128)}) %reduce-scatter.4.cloned.1.call-update) | async-done | bytes 262160
  386.8 1.3 copy.16
  388.1 0.1 neg.6
  388.2 0.3 copy.12
  388.5 0.1 broadcast_multiply_fusion
  388.7 0.0 copy-start.1
  388.7 2.8 fusion
  391.5 0.0 all-reduce.6.cloned.1.call-update
  391.5 0.0 all-reduce.8.cloned.1.call-start
  391.6 140.0 %all-reduce.6.cloned.1.call-done = f32[16,128,128]{2,1,0:T(8,128)} async-done(((f32[16,128,128]{2,1,0:T(8,128)}), f32[16,128,128]{2,1,0:T(8,128)}) %all-reduce.6.cloned.1.call-update) | async-done | bytes 1048592 | tf_op jit(solution)/shard_map/psum | solution.py:40
  531.5 0.0 all-reduce.8.cloned.1.call-update
  531.6 147.5 %all-reduce.8.cloned.1.call-done = f32[16,128,128]{2,1,0:T(8,128)} async-done(((f32[16,128,128]{2,1,0:T(8,128)}), f32[16,128,128]{2,1,0:T(8,128)}) %all-reduce.8.cloned.1.call-update) | async-done | bytes 1048592 | tf_op jit(solution)/shard_map/psum | solution.py:40
  679.1 2.6 sub.10
  681.7 0.0 copy-done.1
  (2 shorter events, 0.0 us)
Async XLA Ops:
  7.2 269.6 %copy-start = (f32[512,512]{1,0:T(8,128)S(1)}, f32[512,512]{1,0:T(8,128)}, u32[]{:S(2)}) copy-start(f32[512,512]{1,0:T(8,128)} %param.4) | copy-start | bytes 3145732
  7.2 68.0 %all-gather.2.cloned.1.call-start = ((), (), s32[]{:S(2)}) async-start(), calls=%async_computation.1 | async-start | bytes 4456448 | tf_op jit(solution)/shard_map/all_gather | solution.py:27
  10.7 266.0 %all-reduce.4.cloned.1.call-start = ((), (), s32[]{:S(2)}) async-start(), calls=%async_computation.2 | async-start | bytes 8388608 | tf_op jit(solution)/shard_map/psum | solution.py:11
  77.7 309.1 %reduce-scatter.4.cloned.1.call-start = ((), (), s32[]{:S(2)}) async-start(), calls=%async_computation.5 | async-start | bytes 4456448
  298.5 233.1 %all-reduce.6.cloned.1.call-start = ((), (), s32[]{:S(2)}) async-start(), calls=%async_computation.3 | async-start | bytes 2097152 | tf_op jit(solution)/shard_map/psum | solution.py:40
  388.7 293.1 %copy-start.1 = (f32[32,16,128]{2,1,0:T(8,128)}, f32[32,16,128]{2,1,0:T(8,128)S(1)}, u32[]{:S(2)}) copy-start(f32[32,16,128]{2,1,0:T(8,128)S(1)} %broadcast_multiply_fusion) | copy-start | bytes 786436
  391.5 287.6 %all-reduce.8.cloned.1.call-start = ((), (), s32[]{:S(2)}) async-start(), calls=%async_computation.4 | async-start | bytes 2097152 | tf_op jit(solution)/shard_map/psum | solution.py:40
Sparse Core Ops, SparseCore 0:
  11.3 63.8 all-gather.1
  77.8 198.8 all-reduce.3
  298.6 88.2 reduce-scatter.3
  391.6 139.8 all-reduce.5
  534.0 145.0 all-reduce.7
